TPU v7x, 128 devices: a whole 4x4x4 slice. The times are simulated.
128 devices in a mesh: grp: 2 (over y_hi), dev: 64 (over x, z, y_lo, core).
Axes of the slice: x: 4, y: 4 (y_hi: 2, y_lo: 2; y = y_hi * 2 + y_lo), z: 4, core: 2. Of those that a mesh axis runs over, the one named last changes fastest.
Arguments:
- multipoles: float32 [2, 384, 41472], P(None, ('grp', 'dev')), may hold values from -6 to 6
- derivatives: float32 [384, 512, 289], P(None, ('grp', 'dev')), may hold values from -0.6666667 to 0.6666667
Outputs:
- taylors: float32 [2, 384, 41472], P(None, ('grp', 'dev'))
All inputs are finite; a program needn't handle non-finite values.
Results may differ from a plain program's by a relative error of at most 0.0001.
Values sent between devices are 32-bit elements; how exact they have to be, the bound alone decides.
A program may use at most 192 MiB of HBM per device.

v0:
```python
import math
import jax
import jax.numpy as jnp
import numpy as np
from jax import lax
from jax.sharding import PartitionSpec as P

ORDER = 8


def reduced_terms(highest):
    listed = []
    for total in range(highest + 1):
        for upper in range(min(total, 1) + 1):
            for first in range(total - upper, -1, -1):
                listed.append((first, total - upper - first, upper))
    return listed


def coupling_matrix(order):
    lower = reduced_terms(order)
    higher = reduced_terms(2 * order)
    where = {}
    for place, triple in enumerate(higher):
        where[triple] = place
    count = len(lower)
    table = np.zeros((len(higher), count * count), np.float32)
    for left, one in enumerate(lower):
        for right, other in enumerate(lower):
            summed = (one[0] + other[0], one[1] + other[1], one[2] + other[2])
            column = left * count + right
            if summed[2] <= 1:
                table[where[summed], column] += 1.0
            else:
                table[where[summed[0] + 2, summed[1], 0], column] -= 1.0
                table[where[summed[0], summed[1] + 2, 0], column] -= 1.0
    return table


def dft_tables(length, positions):
    kvalues = jnp.arange(length, dtype=jnp.int32)
    phase = kvalues[:, None] * positions[None, :] % length
    angle = 2.0 * math.pi / length * phase.astype(jnp.float32)
    factor = 1.0 / math.sqrt(length)
    cosine = jnp.cos(angle) * factor
    sine = jnp.sin(angle) * factor
    forward = jnp.stack([jnp.stack([cosine, sine], 1), jnp.stack([-sine, cosine], 1)], 0)
    inverse = jnp.stack([jnp.stack([cosine.T, -sine.T], 1), jnp.stack([sine.T, cosine.T], 1)], 0)
    return (forward, inverse)


def contract_rows(deriv_rows, spectrum, comp_count):
    table = jnp.asarray(coupling_matrix(ORDER))
    total = deriv_rows.shape[0]
    width = math.gcd(total, 768)
    count = total // width

    def step(index, result):
        start = (index * width).astype(jnp.int32)
        deriv_block = lax.dynamic_slice_in_dim(deriv_rows, start, width, 0)
        coupling = jnp.dot(deriv_block, table, precision=lax.Precision.HIGHEST)
        coupling = coupling.reshape(width, comp_count, comp_count)
        moment_block = lax.dynamic_slice_in_dim(spectrum, start, width, 1)
        block_out = jnp.einsum(
            "pab,rpb->rpa", coupling, moment_block, precision=lax.Precision.HIGHEST
        )
        return lax.dynamic_update_slice_in_dim(result, block_out, start, 1)

    return lax.fori_loop(0, count, step, jnp.zeros(spectrum.shape, spectrum.dtype))


def convolve_group(multipoles, derivatives):
    outer = lax.axis_size("grp")
    inner = lax.axis_size("dev")
    local_rows = multipoles.shape[1]
    length = local_rows * outer * inner
    comp_count = (ORDER + 1) ** 2
    deriv_count = derivatives.shape[2]
    mode_count = derivatives.shape[1]
    row_index = jnp.arange(length, dtype=jnp.int32)
    slab_rows = lax.all_to_all(multipoles, ("grp", "dev"), split_axis=2, concat_axis=1, tiled=True)
    forward, inverse = dft_tables(length, row_index)
    forward_matrix = forward.reshape(2 * length, 2 * length)
    inverse_matrix = inverse.reshape(2 * length, 2 * length)
    matrix = slab_rows.reshape(2 * length, mode_count * comp_count)
    spectrum = jnp.dot(forward_matrix, matrix, precision=lax.Precision.HIGHEST)
    spectrum = spectrum.reshape(2, length * mode_count, comp_count)
    deriv_rows = derivatives.reshape(length * mode_count, deriv_count)
    taylor_k = contract_rows(deriv_rows, spectrum, comp_count)
    taylor_k = taylor_k.reshape(2 * length, mode_count * comp_count)
    returned = jnp.dot(inverse_matrix, taylor_k, precision=lax.Precision.HIGHEST)
    returned = returned.reshape(2, length, mode_count * comp_count)
    result = lax.all_to_all(returned, ("grp", "dev"), split_axis=1, concat_axis=2, tiled=True)
    return result


def on_device(multipoles, derivatives):
    return convolve_group(multipoles, derivatives)


def solution(mesh):
    in_specs = (P(None, ("grp", "dev"), None), P(None, ("grp", "dev"), None))
    out_specs = P(None, ("grp", "dev"), None)
    return jax.shard_map(
        on_device, mesh=mesh, in_specs=in_specs, out_specs=out_specs, check_vma=False
    )
```

profile of v0, /device:TPU:0, one launch (start us, length us, event | category | flops | bytes accessed | tf_op | source)
XLA Modules:
  0.0 560.5 jit_solution(2674592462002672816)
XLA Ops:
  0.0 40.9 %copy.55 = f32[2,3,41472]{1,0,2:T(2,128)} copy(f32[2,3,41472]{2,0,1:T(2,128)} %param.5) | data formatting | bytes 1990656 | tf_op args[0]
  40.9 48.3 %reshape.123 = f32[128,1,1944]{2,1,0:T(1,128)} reshape(f32[41472,2,3]{2,1,0:T(2,128)} %bitcast.37) | data formatting | bytes 1990656
  89.2 11.9 %all-to-all-start = ((f32[128,1,1944]{2,1,0:T(1,128)}), f32[128,1,1944]{2,1,0:T(1,128)}, u32[]{:S(2)}, u32[]{:S(2)}) async-start(f32[128,1,1944]{2,1,0:T(1,128)} %reshape.123), calls=%async_computation | async-start | bytes 2097152 | tf_op jit(solution)/shard_map/all_to_all | solution.py:81
  103.3 2.4 sine_multiply_fusion
  108.5 2.7 copy.53
  117.3 2.5 copy.59
  119.8 3.1 reshape.118
  123.5 4.3 reduce
  127.8 53.6 %reshape.124 = f32[41472,2,3]{2,1,0:T(2,128)} reshape(f32[128,1944]{1,0:T(8,128)S(1)} %reduce) | data formatting | bytes 1990656
  181.5 38.0 %copy.67 = f32[2,3,128,324]{3,2,0,1:T(8,128)S(1)} copy(f32[2,3,128,324]{1,0,3,2:T(2,128)} %bitcast.38) | data formatting | bytes 1990656 | tf_op jit(solution)/shard_map/all_to_all | solution.py:81
  223.2 6.6 %fusion.18 = f32[768,324]{1,0:T(8,128)} fusion(f32[768,768]{1,0:T(8,128)} %bitcast.39, f32[768,324]{1,0:T(8,128)S(1)} %reshape.116), kind=kOutput, calls=%fused_computation.30 | convolution fusion | flops 2293235712 | bytes 4349952 | tf_op jit(solution)/shard_map/dot_general | solution.py:86
  229.8 2.6 reshape.117
  233.7 285.8 %while.14 = (s32[]{:T(128)}, f32[2,1536,81]{2,1,0:T(8,128)}, f32[2,1536,81]{2,1,0:T(8,128)}, f32[1536,289]{1,0:T(8,128)S(1)}, s32[]{:T(128)}, /*index=5*/s32[]{:T(128)}, s32[]{:T(128)}, s32[]{:T(128)}, f32[289,6561]{1,0:T(8,128)}) while((s32[]{:T(128)}, f32[2,1536,81]{2,1,0:T(8,128)}, f32[2,1536,81]{2,1,0:T(8,128)}, ...), condition=%wide.region_1.2_spmd.clone, body=%wide.region_0.1_spmd.sunk.clone.sunk | while | flops 17595656192 | bytes 141222864 | solution.py:69
  233.9 37.5 %fusion.32 = f32[768,6561]{0,1:T(8,128)} fusion(f32[289,6561]{1,0:T(8,128)} %get-tuple-element.202, f32[1536,289]{1,0:T(8,128)S(1)} %get-tuple-element.197, s32[]{:T(128)S(6)} %select_n.65), kind=kOutput, calls=%fused_computation.1.clone.1 | convolution fusion | flops 17474723840 | bytes 28919560 | tf_op jit(solution)/shard_map/while/body/eval_jaxpr/dot_general | solution.py:61
  271.4 17.5 %reshape.126 = f32[768,81,81]{0,2,1:T(8,128)} reshape(f32[768,6561]{0,1:T(8,128)} %fusion.32) | data formatting | bytes 40310784 | tf_op jit(solution)/shard_map/while/body/eval_jaxpr/reshape | solution.py:62
  288.8 27.8 %copy.81 = f32[768,81,81]{2,1,0:T(8,128)} copy(f32[768,81,81]{0,2,1:T(8,128)} %reshape.126) | data formatting | bytes 40310784 | tf_op jit(solution)/shard_map/while/body/eval_jaxpr/reshape | solution.py:62
  317.8 57.5 %convolution_bitcast_fusion.2 = f32[2,768,81]{2,0,1:T(2,128)S(1)} fusion(f32[768,81,81]{2,1,0:T(8,128)} %copy.81, f32[2,768,81]{2,1,0:T(8,128)S(1)} %constant_dynamic-slice_fusion.2), kind=kOutput, calls=%fused_computation.clone.1 | convolution fusion | flops 120932352 | bytes 21150720 | tf_op jit(solution)/shard_map/while/body/eval_jaxpr/pab,rpb->rpa/dot_general | solution.py:64
  376.7 37.4 %fusion.32 = f32[768,6561]{0,1:T(8,128)} fusion(f32[289,6561]{1,0:T(8,128)} %get-tuple-element.202, f32[1536,289]{1,0:T(8,128)S(1)} %get-tuple-element.197, s32[]{:T(128)S(6)} %select_n.65), kind=kOutput, calls=%fused_computation.1.clone.1 | convolution fusion | flops 17474723840 | bytes 28919560 | tf_op jit(solution)/shard_map/while/body/eval_jaxpr/dot_general | solution.py:61
  414.1 17.5 %reshape.126 = f32[768,81,81]{0,2,1:T(8,128)} reshape(f32[768,6561]{0,1:T(8,128)} %fusion.32) | data formatting | bytes 40310784 | tf_op jit(solution)/shard_map/while/body/eval_jaxpr/reshape | solution.py:62
  431.6 27.8 %copy.81 = f32[768,81,81]{2,1,0:T(8,128)} copy(f32[768,81,81]{0,2,1:T(8,128)} %reshape.126) | data formatting | bytes 40310784 | tf_op jit(solution)/shard_map/while/body/eval_jaxpr/reshape | solution.py:62
  460.6 57.5 %convolution_bitcast_fusion.2 = f32[2,768,81]{2,0,1:T(2,128)S(1)} fusion(f32[768,81,81]{2,1,0:T(8,128)} %copy.81, f32[2,768,81]{2,1,0:T(8,128)S(1)} %constant_dynamic-slice_fusion.2), kind=kOutput, calls=%fused_computation.clone.1 | convolution fusion | flops 120932352 | bytes 21150720 | tf_op jit(solution)/shard_map/while/body/eval_jaxpr/pab,rpb->rpa/dot_general | solution.py:64
  521.7 3.7 fusion.4
  527.8 30.1 %all_to_all.33 = f32[2,384,324]{2,0,1:T(2,128)S(1)} all-to-all(f32[2,384,324]{2,0,1:T(2,128)S(1)} %copy.63), channel_id=1, replica_groups=mesh['grp'=2,'dev'=64] {'grp','dev'}, dimensions={1} | all-to-all | bytes 1990656 | tf_op jit(solution)/shard_map/all_to_all | solution.py:93
  557.9 2.4 all_to_all.30
  (36 shorter events, 26.0 us)
Async XLA Ops:
  89.2 33.7 %all-to-all-start = ((f32[128,1,1944]{2,1,0:T(1,128)}), f32[128,1,1944]{2,1,0:T(1,128)}, u32[]{:S(2)}, u32[]{:S(2)}) async-start(f32[128,1,1944]{2,1,0:T(1,128)} %reshape.123), calls=%async_computation | async-start | bytes 2097152 | tf_op jit(solution)/shard_map/all_to_all | solution.py:81
  111.6 1.4 copy-start.2
  115.0 2.3 copy-start.5
  317.8 57.6 %copy-start = (f32[2,1536,81]{2,1,0:T(8,128)S(1)}, f32[2,1536,81]{2,1,0:T(8,128)}, u32[]{:S(2)}) copy-start(f32[2,1536,81]{2,1,0:T(8,128)} %get-tuple-element.186) | copy-start | bytes 2985988 | tf_op jit(solution)/shard_map/while
  375.5 1.2 copy-start.1
  460.6 57.6 %copy-start = (f32[2,1536,81]{2,1,0:T(8,128)S(1)}, f32[2,1536,81]{2,1,0:T(8,128)}, u32[]{:S(2)}) copy-start(f32[2,1536,81]{2,1,0:T(8,128)} %get-tuple-element.186) | copy-start | bytes 2985988 | tf_op jit(solution)/shard_map/while
  518.2 1.2 copy-start.1
  519.6 2.0 copy-start.3
  519.6 2.1 copy-start.4
where the time goes:
time: 570 us; the launch traced here: 561 us
  local copies, waits for them, and re-layouts  307 us (54%)
  matrix products  200 us (35%)
  blocking collectives  30.1 us (5%)
  starting transfers between devices  11.9 us (2%)
  other arithmetic  10.5 us (2%)
    unnamed x13, local copies, waits for them, and re-layouts  148 us
    dot_general x2, matrix products, step(): jnp.einsum('pab,rpb->rpa', coupling, moment_block, precision=lax.Precisio...  115 us
    reshape x4, local copies, waits for them, and re-layouts, step(): coupling = coupling.reshape(width, comp_count, comp_count)  90.5 us
    dot_general x2, matrix products, step(): coupling = jnp.dot(deriv_block, table, precision=lax.Precision.HIGHEST)  74.9 us
    all_to_all x3, local copies, waits for them, and re-layouts, convolve_group(): lax.all_to_all(multipoles, ('grp', 'dev'), split_axis=2, concat_axis=1, t...  40.6 us
    all_to_all x1, blocking collectives, convolve_group(): lax.all_to_all(returned, ('grp', 'dev'), split_axis=1, concat_axis=2, til...  30.1 us
    all_to_all x1, starting transfers between devices, convolve_group(): lax.all_to_all(multipoles, ('grp', 'dev'), split_axis=2, concat_axis=1, t...  11.9 us
  transfers between devices with their start and end apart: 1, of which 0 were waited for; matrix products, arithmetic and copies ran while one was open for 4% of the time, Pallas kernels for 0%

commit v1 on v0

--- a/solution.py
+++ b/solution.py
@@ -78,7 +78,15 @@
     deriv_count = derivatives.shape[2]
     mode_count = derivatives.shape[1]
     row_index = jnp.arange(length, dtype=jnp.int32)
-    slab_rows = lax.all_to_all(multipoles, ("grp", "dev"), split_axis=2, concat_axis=1, tiled=True)
+    slab_rows = jnp.concatenate(
+        lax.all_to_all(
+            jnp.stack(jnp.split(multipoles, lax.axis_size(("grp", "dev")), axis=2)),
+            ("grp", "dev"),
+            0,
+            0,
+        ),
+        axis=1,
+    )
     forward, inverse = dft_tables(length, row_index)
     forward_matrix = forward.reshape(2 * length, 2 * length)
     inverse_matrix = inverse.reshape(2 * length, 2 * length)

time: 570 us -> 514 us (0.902)
  local copies, waits for them, and re-layouts: 307 us -> 257 us
    all_to_all x3 -> x0, local copies, waits for them, and re-layouts: 40.6 us -> none  [convolve_group(): lax.all_to_all(multipoles, ('grp', 'dev'), split_axis=2, concat_axis=1, t...]
    unnamed x13 -> x139, local copies, waits for them, and re-layouts: 148 us -> 136 us
where the time goes in v1:
time: 514 us; the launch traced here: 506 us
  local copies, waits for them, and re-layouts  257 us (50%)
  matrix products  200 us (39%)
  blocking collectives  30.1 us (6%)
  starting transfers between devices  11.8 us (2%)
  other arithmetic  6.16 us (1%)
    unnamed x139, local copies, waits for them, and re-layouts  136 us
    dot_general x2, matrix products, step(): jnp.einsum('pab,rpb->rpa', coupling, moment_block, precision=lax.Precisio...  115 us
    reshape x4, local copies, waits for them, and re-layouts, step(): coupling = coupling.reshape(width, comp_count, comp_count)  90.4 us
    dot_general x2, matrix products, step(): coupling = jnp.dot(deriv_block, table, precision=lax.Precision.HIGHEST)  74.9 us
    all_to_all x1, blocking collectives, convolve_group(): lax.all_to_all(returned, ('grp', 'dev'), split_axis=1, concat_axis=2, til...  30.1 us
    all_to_all x1, starting transfers between devices, convolve_group(): lax.all_to_all(jnp.stack(jnp.split(multipoles, lax.axis_size(('grp', 'dev...  11.8 us
  transfers between devices with their start and end apart: 1, of which 0 were waited for; matrix products, arithmetic and copies ran while one was open for 4% of the time, Pallas kernels for 0%

profile of v1, /device:TPU:0, one launch (start us, length us, event | category | flops | bytes accessed | tf_op | source)
XLA Modules:
  0.0 506.4 jit_solution(17329579955231167222)
XLA Ops:
  131.3 11.8 %all-to-all-start = ((f32[128,2,3,324]{3,1,2,0:T(2,128)}), f32[128,2,3,324]{3,1,2,0:T(2,128)}, u32[]{:S(2)}, u32[]{:S(2)}) async-start(f32[128,2,3,324]{3,1,2,0:T(2,128)} %constant_dynamic-update-slice_fusion), calls=%async_computation | async-start | bytes 2359296 | tf_op jit(solution)/shard_map/all_to_all | solution.py:82
  143.2 2.3 fusion.16
  145.4 2.4 sine_multiply_fusion
  150.6 2.7 copy.38
  155.2 1.8 copy.39
  159.4 2.5 copy.42
  161.9 2.7 reshape.117
  164.6 2.8 copy.40
  169.1 6.6 %fusion.18 = f32[768,324]{1,0:T(8,128)} fusion(f32[768,768]{1,0:T(8,128)} %bitcast.290, f32[768,324]{1,0:T(8,128)S(1)} %reshape_reshape.3), kind=kOutput, calls=%fused_computation.158 | convolution fusion | flops 2293235712 | bytes 4349952 | tf_op jit(solution)/shard_map/dot_general | solution.py:94
  175.7 2.6 reshape.116
  179.6 285.9 %while.14 = (s32[]{:T(128)}, f32[2,1536,81]{2,1,0:T(8,128)}, f32[2,1536,81]{2,1,0:T(8,128)}, f32[1536,289]{1,0:T(8,128)S(1)}, s32[]{:T(128)}, /*index=5*/s32[]{:T(128)}, s32[]{:T(128)}, s32[]{:T(128)}, f32[289,6561]{1,0:T(8,128)}) while((s32[]{:T(128)}, f32[2,1536,81]{2,1,0:T(8,128)}, f32[2,1536,81]{2,1,0:T(8,128)}, ...), condition=%wide.region_1.2_spmd.clone, body=%wide.region_0.1_spmd.sunk.clone.sunk | while | flops 17595656192 | bytes 141222864 | solution.py:69
  180.0 37.5 %fusion.32 = f32[768,6561]{0,1:T(8,128)} fusion(f32[289,6561]{1,0:T(8,128)} %get-tuple-element.198, f32[1536,289]{1,0:T(8,128)S(1)} %get-tuple-element.193, s32[]{:T(128)S(6)} %select_n.65), kind=kOutput, calls=%fused_computation.1.clone.1 | convolution fusion | flops 17474723840 | bytes 28919560 | tf_op jit(solution)/shard_map/while/body/eval_jaxpr/dot_general | solution.py:61
  217.5 17.5 %reshape.123 = f32[768,81,81]{0,2,1:T(8,128)} reshape(f32[768,6561]{0,1:T(8,128)} %fusion.32) | data formatting | bytes 40310784 | tf_op jit(solution)/shard_map/while/body/eval_jaxpr/reshape | solution.py:62
  234.9 27.7 %copy.63 = f32[768,81,81]{2,1,0:T(8,128)} copy(f32[768,81,81]{0,2,1:T(8,128)} %reshape.123) | data formatting | bytes 40310784 | tf_op jit(solution)/shard_map/while/body/eval_jaxpr/reshape | solution.py:62
  263.8 57.5 %convolution_bitcast_fusion.2 = f32[2,768,81]{2,0,1:T(2,128)S(1)} fusion(f32[768,81,81]{2,1,0:T(8,128)} %copy.63, f32[2,768,81]{2,1,0:T(8,128)S(1)} %constant_dynamic-slice_fusion.2), kind=kOutput, calls=%fused_computation.clone.1 | convolution fusion | flops 120932352 | bytes 21150720 | tf_op jit(solution)/shard_map/while/body/eval_jaxpr/pab,rpb->rpa/dot_general | solution.py:64
  322.7 37.5 %fusion.32 = f32[768,6561]{0,1:T(8,128)} fusion(f32[289,6561]{1,0:T(8,128)} %get-tuple-element.198, f32[1536,289]{1,0:T(8,128)S(1)} %get-tuple-element.193, s32[]{:T(128)S(6)} %select_n.65), kind=kOutput, calls=%fused_computation.1.clone.1 | convolution fusion | flops 17474723840 | bytes 28919560 | tf_op jit(solution)/shard_map/while/body/eval_jaxpr/dot_general | solution.py:61
  360.1 17.5 %reshape.123 = f32[768,81,81]{0,2,1:T(8,128)} reshape(f32[768,6561]{0,1:T(8,128)} %fusion.32) | data formatting | bytes 40310784 | tf_op jit(solution)/shard_map/while/body/eval_jaxpr/reshape | solution.py:62
  377.6 27.7 %copy.63 = f32[768,81,81]{2,1,0:T(8,128)} copy(f32[768,81,81]{0,2,1:T(8,128)} %reshape.123) | data formatting | bytes 40310784 | tf_op jit(solution)/shard_map/while/body/eval_jaxpr/reshape | solution.py:62
  406.5 57.5 %convolution_bitcast_fusion.2 = f32[2,768,81]{2,0,1:T(2,128)S(1)} fusion(f32[768,81,81]{2,1,0:T(8,128)} %copy.63, f32[2,768,81]{2,1,0:T(8,128)S(1)} %constant_dynamic-slice_fusion.2), kind=kOutput, calls=%fused_computation.clone.1 | convolution fusion | flops 120932352 | bytes 21150720 | tf_op jit(solution)/shard_map/while/body/eval_jaxpr/pab,rpb->rpa/dot_general | solution.py:64
  465.5 2.0 reshape.118
  467.6 3.7 fusion.4
  471.3 2.4 copy.46
  473.7 30.1 %all_to_all.23 = f32[2,384,324]{2,0,1:T(2,128)S(1)} all-to-all(f32[2,384,324]{2,0,1:T(2,128)S(1)} %copy.46), channel_id=1, replica_groups=mesh['grp'=2,'dev'=64] {'grp','dev'}, dimensions={1} | all-to-all | bytes 1990656 | tf_op jit(solution)/shard_map/all_to_all | solution.py:101
  503.8 2.4 all_to_all.20
  (160 shorter events, 146.3 us)
Async XLA Ops:
  0.0 88.3 %copy-start.6 = (f32[2,3,41472]{2,0,1:T(2,128)S(1)}, f32[2,3,41472]{2,0,1:T(2,128)}, u32[]{:S(2)}) copy-start(f32[2,3,41472]{2,0,1:T(2,128)} %param.5) | copy-start | bytes 2985988
  131.3 33.2 %all-to-all-start = ((f32[128,2,3,324]{3,1,2,0:T(2,128)}), f32[128,2,3,324]{3,1,2,0:T(2,128)}, u32[]{:S(2)}, u32[]{:S(2)}) async-start(f32[128,2,3,324]{3,1,2,0:T(2,128)} %constant_dynamic-update-slice_fusion), calls=%async_computation | async-start | bytes 2359296 | tf_op jit(solution)/shard_map/all_to_all | solution.py:82
  153.7 1.4 copy-start.2
  157.0 2.3 copy-start.5
  263.8 57.6 %copy-start = (f32[2,1536,81]{2,1,0:T(8,128)S(1)}, f32[2,1536,81]{2,1,0:T(8,128)}, u32[]{:S(2)}) copy-start(f32[2,1536,81]{2,1,0:T(8,128)} %get-tuple-element.182) | copy-start | bytes 2985988 | tf_op jit(solution)/shard_map/while
  321.5 1.2 copy-start.1
  406.5 57.6 %copy-start = (f32[2,1536,81]{2,1,0:T(8,128)S(1)}, f32[2,1536,81]{2,1,0:T(8,128)}, u32[]{:S(2)}) copy-start(f32[2,1536,81]{2,1,0:T(8,128)} %get-tuple-element.182) | copy-start | bytes 2985988 | tf_op jit(solution)/shard_map/while
  464.2 1.2 copy-start.1
  465.5 2.0 copy-start.3
  465.5 2.1 copy-start.4
